TPU v7x, 512 devices: a whole 4x4x16 slice. The times are simulated.
512 devices in a mesh: spec: 16 (over y, x), tile: 32 (over z, core).
Axes of the slice: x: 4, y: 4, z: 16, core: 2. Of those that a mesh axis runs over, the one named last changes fastest.
Arguments:
- action: bfloat16 [512, 3072, 256], P('tile', 'spec'), may hold values from 0.099609375 to 2
- east_current: float32 [512, 256], P('tile'), may hold values from -0.4 to 0.4
- north_current: float32 [512, 256], P('tile'), may hold values from -0.4 to 0.4
- sea_mask: int32 [512, 256], P('tile'), may hold values from 0 to 1, as said below
- pattern: int32 [48, 24], replicated, may hold values from 0 to 47, as said below
- table: bfloat16 [48, 64, 64], replicated, may hold values from -0.15625 to 0.15625
Outputs:
- updated: bfloat16 [512, 3072, 256], P('tile', 'spec')
Inputs may be any that keep to these rules, and one draw needn't show every extreme that they name: `sea_mask`: each tile of 16 latitude rows (all 256 longitudes) holds at most 2048 sea points, and in every draw some tile holds exactly 2048. `pattern`: each row names 24 different direction blocks.
All inputs are finite; a program needn't handle non-finite values.
Results may differ from a plain program's by a relative error of at most 0.0043.
Values may be sent and summed in bfloat16 or wider, within the bound.
A program may use at most 64 MiB of HBM per device.

v0:
```python
import jax
import jax.numpy as jnp
from jax import lax
from jax.sharding import PartitionSpec as P

NF = 64
ND = 48
SUB = 2


courant_scale = 0.45


def extended(cells, sides, width):
    for axis, dim in sides:
        count = lax.axis_size(axis)
        ends = count - 1
        head = lax.slice_in_dim(cells, 0, width, axis=dim)
        tail = lax.slice_in_dim(cells, cells.shape[dim] - width, cells.shape[dim], axis=dim)
        cells = jnp.concatenate(
            [
                lax.ppermute(tail, axis, [(i, (i + 1) % count) for i in range(ends)]),
                cells,
                lax.ppermute(head, axis, [((i + 1) % count, i) for i in range(ends)]),
            ],
            axis=dim,
        )
    return cells


def upwind(padded, courant_east, courant_north):
    center = padded[1:-1]
    south_row = padded[:-2]
    north_row = padded[2:]
    zero_column = jnp.zeros_like(center[:, :, :1])
    west_cell = jnp.concatenate([zero_column, center[:, :, :-1]], axis=2)
    east_cell = jnp.concatenate([center[:, :, 1:], zero_column], axis=2)
    return (
        center
        - jnp.maximum(courant_east, 0.0) * (center - west_cell)
        - jnp.minimum(courant_east, 0.0) * (east_cell - center)
        - jnp.maximum(courant_north, 0.0) * (center - south_row)
        - jnp.minimum(courant_north, 0.0) * (north_row - center)
    )


def source_update(cell_action, cell_mask, pattern, table):
    row_count = cell_action.shape[0]
    lane_count = cell_action.shape[2]
    group_size = 8
    offsets = (pattern - jnp.arange(ND, dtype=jnp.int32)[:, None]) % ND
    directions = jnp.arange(ND, dtype=jnp.int32)

    def advance_group(unused_state, group_rows):
        selector = (pattern[group_rows][:, :, None] == directions[None, None, :]).astype(
            jnp.float32
        )
        weights = table[offsets[group_rows]].astype(jnp.float32)
        assembled = jnp.einsum("rjc,rjab->racb", selector, weights)
        assembled = assembled.astype(jnp.bfloat16).reshape(group_size * NF, ND * NF)
        coupled = jnp.einsum(
            "ak,rkl->ral", assembled, cell_action, preferred_element_type=jnp.float32
        )
        return (unused_state, coupled)

    group_index = directions.reshape(ND // group_size, group_size)
    unused_state, coupled = lax.scan(advance_group, jnp.zeros((), jnp.float32), group_index)
    coupled = jnp.transpose(coupled, (1, 0, 2, 3)).reshape(row_count, ND * NF, lane_count)
    own_action = cell_action.astype(jnp.float32)
    sea_part = cell_mask.astype(jnp.float32)[:, None, :]
    result = own_action + sea_part * own_action * coupled
    return result.astype(jnp.bfloat16)


def local(action, east_current, north_current, sea_mask, pattern, table):
    tile_rows = action.shape[0]
    comp_count = action.shape[1]
    spec_count = lax.axis_size("spec")
    spec_index = lax.axis_index("spec")
    components = spec_index * comp_count + jnp.arange(comp_count, dtype=jnp.int32)
    direction = (components // NF).astype(jnp.float32)
    frequency = (components % NF).astype(jnp.float32)
    speed = jnp.exp(-2.0 * frequency / (NF - 1))
    theta = 2.0 * jnp.pi * direction / ND
    courant_east = courant_scale * (
        (speed * jnp.cos(theta))[None, :, None] + east_current[:, None, :]
    )
    courant_north = courant_scale * (
        (speed * jnp.sin(theta))[None, :, None] + north_current[:, None, :]
    )
    field = action.astype(jnp.float32)
    for substep in range(SUB):
        padded = extended(field, (("tile", 0),), 1)
        field = upwind(padded, courant_east, courant_north)
    moved = field.astype(jnp.bfloat16)
    share_rows = tile_rows // spec_count
    incoming = lax.all_to_all(moved, "spec", split_axis=0, concat_axis=1, tiled=True)
    own_mask = lax.dynamic_slice_in_dim(sea_mask, spec_index * share_rows, share_rows, 0)
    renewed = source_update(incoming, own_mask, pattern, table)
    result = lax.all_to_all(renewed, "spec", split_axis=1, concat_axis=0, tiled=True)
    return result


def solution(mesh):
    return jax.shard_map(
        local,
        mesh=mesh,
        in_specs=(
            P("tile", "spec", None),
            P("tile", None),
            P("tile", None),
            P("tile", None),
            P(),
            P(),
        ),
        out_specs=P("tile", "spec", None),
        check_vma=False,
    )
```

profile of v0, /device:TPU:416, one launch (start us, length us, event | category | flops | bytes accessed | tf_op | source)
XLA Modules:
  0.0 262.7 jit_solution(9454348573724922030)
XLA Ops:
  2.9 3.8 %collective-permute-start.1 = (f32[1,192,256]{2,1,0:T(8,128)S(1)}, f32[1,192,256]{2,1,0:T(8,128)S(1)}, u32[]{:S(2)}, u32[]{:S(2)}) collective-permute-start(f32[1,192,256]{2,1,0:T(8,128)S(1)} %get-tuple-element.106), channel_id=1, source_target_pairs={{1,0},{2,1},{3,2},{4,3},{5,4},{6,5},{7,6},{8,7},{9,8},{10,9},{11,1... | collective-permute-start | bytes 589832 | tf_op jit(solution)/shard_map/ppermute | solution.py:24
  6.7 5.5 %fusion.41 = (f32[16,192,255]{2,1,0:T(8,128)}, f32[16,192,255]{2,1,0:T(8,128)}) fusion(bf16[16,192,256]{2,1,0:T(8,128)(2,1)} %param.8), kind=kLoop, calls=%fused_computation.71 | loop fusion | bytes 12533760 | tf_op jit(solution)/shard_map/slice | solution.py:36
  14.3 5.8 %fusion.18 = f32[16,192,256]{2,1,0:T(8,128)S(1)} fusion(bf16[16,192,256]{2,1,0:T(8,128)(2,1)S(1)} %copy-done, f32[1,192,256]{2,1,0:T(8,128)S(1)} %collective-permute-done.1, f32[16,192,256]{2,1,0:T(8,128)} %convert_element_type.59, f32[1,192,256]{2,1,0:T(8,128)S(1)} %collective-permute-done, f32[16,192,255]{2,1,0:T(8,128)} %get-tuple-element.104, ...), kind=kLoop, calls=%fused_computation.28 | loop fusion | flops 18087936 | bytes 14558720 | tf_op jit(solution)/shard_map/sub | solution.py:39
  22.1 3.6 %collective-permute-start.3 = (f32[1,192,256]{2,1,0:T(8,128)S(1)}, f32[1,192,256]{2,1,0:T(8,128)S(1)}, u32[]{:S(2)}, u32[]{:S(2)}) collective-permute-start(f32[1,192,256]{2,1,0:T(8,128)S(1)} %get-tuple-element.102), channel_id=1, source_target_pairs={{1,0},{2,1},{3,2},{4,3},{5,4},{6,5},{7,6},{8,7},{9,8},{10,9},{11,1... | collective-permute-start | bytes 589832 | tf_op jit(solution)/shard_map/ppermute | solution.py:24
  28.9 3.9 %fusion.27 = bf16[16,192,256]{2,1,0:T(8,128)(2,1)} fusion(f32[16,192,256]{2,1,0:T(8,128)S(1)} %fusion.18, f32[1,192,256]{2,1,0:T(8,128)S(1)} %collective-permute-done.3, f32[1,192,256]{2,1,0:T(8,128)S(1)} %collective-permute-done.2, f32[16,192,255]{2,1,0:T(8,128)S(1)} %get-tuple-element.100, f32[16,192,255]{2,1,0:T(8,128)S(1)} %get-tuple-element.99, ...), kind=kLoop, calls=%fused_computation.38 | loop fusion | flops 18087936 | bytes 11412992 | tf_op jit(solution)/shard_map/convert_element_type | solution.py:95
  32.8 7.2 %all-to-all-start = ((bf16[16,192,256]{2,1,0:T(8,128)(2,1)}), bf16[16,192,256]{2,1,0:T(8,128)(2,1)}, u32[]{:S(2)}, u32[]{:S(2)}) async-start(bf16[16,192,256]{2,1,0:T(8,128)(2,1)} %fusion.27), calls=%async_computation | async-start | bytes 3145728 | tf_op jit(solution)/shard_map/all_to_all | solution.py:97
  40.9 27.2 %all-to-all-done = bf16[16,192,256]{2,1,0:T(8,128)(2,1)} async-done(((bf16[16,192,256]{2,1,0:T(8,128)(2,1)}), bf16[16,192,256]{2,1,0:T(8,128)(2,1)}, u32[]{:S(2)}, u32[]{:S(2)}) %all-to-all-start) | async-done | bytes 1572896 | tf_op jit(solution)/shard_map/all_to_all | solution.py:97
  68.0 117.2 %while.11 = (s32[]{:T(128)}, f32[6,1,512,256]{3,2,1,0:T(8,128)}, s32[6,8]{1,0:T(8,128)S(1)}, s32[48,24]{1,0:T(8,128)S(1)}, bf16[48,64,64]{2,1,0:T(8,128)(2,1)}, ...) while((s32[]{:T(128)}, f32[6,1,512,256]{3,2,1,0:T(8,128)}, ...), condition=%wide.region_1.2_spmd.clone, body=%wide.region_0.1_spmd.clone.sunk | while | flops 882388544 | bytes 19416056 | solution.py:67
  71.6 5.3 %convert_bitcast_fusion.2 = bf16[8,64,48,64]{3,2,1,0:T(8,128)(2,1)} fusion(bf16[8,24,64,64]{3,2,1,0:T(8,128)(2,1)S(1)} %bitcast.64, s32[8,24]{1,0:T(8,128)S(1)} %gather_fusion.2), kind=kOutput, calls=%fused_computation.4.clone.1 | convolution fusion | flops 77079552 | bytes 4719360 | tf_op jit(solution)/shard_map/while/body/eval_jaxpr/rjc,rjab->racb/dot_general | solution.py:59
  76.8 7.5 %reshape.229 = bf16[512,3072]{1,0:T(8,128)(2,1)S(1)} reshape(bf16[8,64,48,64]{3,2,1,0:T(8,128)(2,1)} %convert_bitcast_fusion.2) | data formatting | bytes 6291456 | tf_op jit(solution)/shard_map/while/body/eval_jaxpr/reshape | solution.py:60
  84.4 3.2 %fusion.55 = f32[6,1,512,256]{3,2,1,0:T(8,128)} fusion(f32[6,1,512,256]{3,2,1,0:T(8,128)} %get-tuple-element.161, s32[]{:T(128)} %get-tuple-element.160, bf16[512,3072]{1,0:T(8,128)(2,1)S(1)} %reshape.229, bf16[1,3072,256]{2,1,0:T(8,128)(2,1)} %get-tuple-element.174), kind=kOutput, calls=%fused_computation.9.clone.1 | convolution fusion | flops 805306368 | bytes 5243392 | tf_op jit(solution)/shard_map/while/body/eval_jaxpr/ak,rkl->ral/dot_general | solution.py:61
  91.1 5.3 %convert_bitcast_fusion.2 = bf16[8,64,48,64]{3,2,1,0:T(8,128)(2,1)} fusion(bf16[8,24,64,64]{3,2,1,0:T(8,128)(2,1)S(1)} %bitcast.64, s32[8,24]{1,0:T(8,128)S(1)} %gather_fusion.2), kind=kOutput, calls=%fused_computation.4.clone.1 | convolution fusion | flops 77079552 | bytes 4719360 | tf_op jit(solution)/shard_map/while/body/eval_jaxpr/rjc,rjab->racb/dot_general | solution.py:59
  96.4 7.5 %reshape.229 = bf16[512,3072]{1,0:T(8,128)(2,1)S(1)} reshape(bf16[8,64,48,64]{3,2,1,0:T(8,128)(2,1)} %convert_bitcast_fusion.2) | data formatting | bytes 6291456 | tf_op jit(solution)/shard_map/while/body/eval_jaxpr/reshape | solution.py:60
  103.9 3.2 %fusion.55 = f32[6,1,512,256]{3,2,1,0:T(8,128)} fusion(f32[6,1,512,256]{3,2,1,0:T(8,128)} %get-tuple-element.161, s32[]{:T(128)} %get-tuple-element.160, bf16[512,3072]{1,0:T(8,128)(2,1)S(1)} %reshape.229, bf16[1,3072,256]{2,1,0:T(8,128)(2,1)} %get-tuple-element.174), kind=kOutput, calls=%fused_computation.9.clone.1 | convolution fusion | flops 805306368 | bytes 5243392 | tf_op jit(solution)/shard_map/while/body/eval_jaxpr/ak,rkl->ral/dot_general | solution.py:61
  110.6 5.3 %convert_bitcast_fusion.2 = bf16[8,64,48,64]{3,2,1,0:T(8,128)(2,1)} fusion(bf16[8,24,64,64]{3,2,1,0:T(8,128)(2,1)S(1)} %bitcast.64, s32[8,24]{1,0:T(8,128)S(1)} %gather_fusion.2), kind=kOutput, calls=%fused_computation.4.clone.1 | convolution fusion | flops 77079552 | bytes 4719360 | tf_op jit(solution)/shard_map/while/body/eval_jaxpr/rjc,rjab->racb/dot_general | solution.py:59
  115.9 7.5 %reshape.229 = bf16[512,3072]{1,0:T(8,128)(2,1)S(1)} reshape(bf16[8,64,48,64]{3,2,1,0:T(8,128)(2,1)} %convert_bitcast_fusion.2) | data formatting | bytes 6291456 | tf_op jit(solution)/shard_map/while/body/eval_jaxpr/reshape | solution.py:60
  123.4 3.2 %fusion.55 = f32[6,1,512,256]{3,2,1,0:T(8,128)} fusion(f32[6,1,512,256]{3,2,1,0:T(8,128)} %get-tuple-element.161, s32[]{:T(128)} %get-tuple-element.160, bf16[512,3072]{1,0:T(8,128)(2,1)S(1)} %reshape.229, bf16[1,3072,256]{2,1,0:T(8,128)(2,1)} %get-tuple-element.174), kind=kOutput, calls=%fused_computation.9.clone.1 | convolution fusion | flops 805306368 | bytes 5243392 | tf_op jit(solution)/shard_map/while/body/eval_jaxpr/ak,rkl->ral/dot_general | solution.py:61
  130.1 5.3 %convert_bitcast_fusion.2 = bf16[8,64,48,64]{3,2,1,0:T(8,128)(2,1)} fusion(bf16[8,24,64,64]{3,2,1,0:T(8,128)(2,1)S(1)} %bitcast.64, s32[8,24]{1,0:T(8,128)S(1)} %gather_fusion.2), kind=kOutput, calls=%fused_computation.4.clone.1 | convolution fusion | flops 77079552 | bytes 4719360 | tf_op jit(solution)/shard_map/while/body/eval_jaxpr/rjc,rjab->racb/dot_general | solution.py:59
  135.4 7.5 %reshape.229 = bf16[512,3072]{1,0:T(8,128)(2,1)S(1)} reshape(bf16[8,64,48,64]{3,2,1,0:T(8,128)(2,1)} %convert_bitcast_fusion.2) | data formatting | bytes 6291456 | tf_op jit(solution)/shard_map/while/body/eval_jaxpr/reshape | solution.py:60
  142.9 3.2 %fusion.55 = f32[6,1,512,256]{3,2,1,0:T(8,128)} fusion(f32[6,1,512,256]{3,2,1,0:T(8,128)} %get-tuple-element.161, s32[]{:T(128)} %get-tuple-element.160, bf16[512,3072]{1,0:T(8,128)(2,1)S(1)} %reshape.229, bf16[1,3072,256]{2,1,0:T(8,128)(2,1)} %get-tuple-element.174), kind=kOutput, calls=%fused_computation.9.clone.1 | convolution fusion | flops 805306368 | bytes 5243392 | tf_op jit(solution)/shard_map/while/body/eval_jaxpr/ak,rkl->ral/dot_general | solution.py:61
  149.6 5.3 %convert_bitcast_fusion.2 = bf16[8,64,48,64]{3,2,1,0:T(8,128)(2,1)} fusion(bf16[8,24,64,64]{3,2,1,0:T(8,128)(2,1)S(1)} %bitcast.64, s32[8,24]{1,0:T(8,128)S(1)} %gather_fusion.2), kind=kOutput, calls=%fused_computation.4.clone.1 | convolution fusion | flops 77079552 | bytes 4719360 | tf_op jit(solution)/shard_map/while/body/eval_jaxpr/rjc,rjab->racb/dot_general | solution.py:59
  154.9 7.5 %reshape.229 = bf16[512,3072]{1,0:T(8,128)(2,1)S(1)} reshape(bf16[8,64,48,64]{3,2,1,0:T(8,128)(2,1)} %convert_bitcast_fusion.2) | data formatting | bytes 6291456 | tf_op jit(solution)/shard_map/while/body/eval_jaxpr/reshape | solution.py:60
  162.4 3.2 %fusion.55 = f32[6,1,512,256]{3,2,1,0:T(8,128)} fusion(f32[6,1,512,256]{3,2,1,0:T(8,128)} %get-tuple-element.161, s32[]{:T(128)} %get-tuple-element.160, bf16[512,3072]{1,0:T(8,128)(2,1)S(1)} %reshape.229, bf16[1,3072,256]{2,1,0:T(8,128)(2,1)} %get-tuple-element.174), kind=kOutput, calls=%fused_computation.9.clone.1 | convolution fusion | flops 805306368 | bytes 5243392 | tf_op jit(solution)/shard_map/while/body/eval_jaxpr/ak,rkl->ral/dot_general | solution.py:61
  169.2 5.3 %convert_bitcast_fusion.2 = bf16[8,64,48,64]{3,2,1,0:T(8,128)(2,1)} fusion(bf16[8,24,64,64]{3,2,1,0:T(8,128)(2,1)S(1)} %bitcast.64, s32[8,24]{1,0:T(8,128)S(1)} %gather_fusion.2), kind=kOutput, calls=%fused_computation.4.clone.1 | convolution fusion | flops 77079552 | bytes 4719360 | tf_op jit(solution)/shard_map/while/body/eval_jaxpr/rjc,rjab->racb/dot_general | solution.py:59
  174.5 7.5 %reshape.229 = bf16[512,3072]{1,0:T(8,128)(2,1)S(1)} reshape(bf16[8,64,48,64]{3,2,1,0:T(8,128)(2,1)} %convert_bitcast_fusion.2) | data formatting | bytes 6291456 | tf_op jit(solution)/shard_map/while/body/eval_jaxpr/reshape | solution.py:60
  182.0 3.2 %fusion.55 = f32[6,1,512,256]{3,2,1,0:T(8,128)} fusion(f32[6,1,512,256]{3,2,1,0:T(8,128)} %get-tuple-element.161, s32[]{:T(128)} %get-tuple-element.160, bf16[512,3072]{1,0:T(8,128)(2,1)S(1)} %reshape.229, bf16[1,3072,256]{2,1,0:T(8,128)(2,1)} %get-tuple-element.174), kind=kOutput, calls=%fused_computation.9.clone.1 | convolution fusion | flops 805306368 | bytes 5243392 | tf_op jit(solution)/shard_map/while/body/eval_jaxpr/ak,rkl->ral/dot_general | solution.py:61
  185.2 2.8 %fusion.23 = bf16[1,3072,256]{2,1,0:T(8,128)(2,1)S(1)} fusion(f32[1,3072,256]{2,1,0:T(8,128)} %bitcast.67, f32[256]{0:T(256)S(1)} %bitcast.68, bf16[1,3072,256]{2,1,0:T(8,128)(2,1)} %bitcast.45), kind=kLoop, calls=%fused_computation.33 | loop fusion | flops 3932160 | bytes 6292480 | tf_op jit(solution)/shard_map/convert_element_type | solution.py:72
  188.0 17.5 %copy.23 = bf16[1,3072,256]{2,0,1:T(2,128)(2,1)S(1)} copy(bf16[1,3072,256]{2,1,0:T(8,128)(2,1)S(1)} %fusion.23) | data formatting | bytes 3145728 | tf_op jit(solution)/shard_map/convert_element_type | solution.py:72
  206.1 16.6 %reduce = bf16[3072,256]{1,0:T(8,128)(2,1)} reduce(bf16[3072,1,256]{2,1,0:T(2,128)(2,1)S(1)} %bitcast.65, bf16[]{:T(256)} %broadcast.244), dimensions={1}, to_apply=%bitcast.44.reduce_sub_computation | reduce | bytes 3145730
  222.7 3.7 %reshape.212 = bf16[16,2,24576]{2,1,0:T(2,128)(2,1)S(1)} reshape(bf16[3072,256]{1,0:T(8,128)(2,1)} %reduce) | data formatting | bytes 3145728
  226.5 26.7 %all_to_all.24 = bf16[16,2,24576]{2,1,0:T(2,128)(2,1)} all-to-all(bf16[16,2,24576]{2,1,0:T(2,128)(2,1)S(1)} %reshape.212), channel_id=1, replica_groups=mesh['spec'=16,'tile'=32] {'spec'}, dimensions={0} | all-to-all | bytes 3145728 | tf_op jit(solution)/shard_map/all_to_all | solution.py:100
  253.2 8.1 %reshape.213 = bf16[3072,1,256]{2,1,0:T(2,128)(2,1)S(1)} reshape(bf16[16,2,24576]{2,1,0:T(2,128)(2,1)} %all_to_all.24) | data formatting | bytes 3145728
  (74 shorter events, 33.9 us)
Async XLA Ops:
  1.0 13.2 %collective-permute-start = (f32[1,192,256]{2,1,0:T(8,128)S(1)}, f32[1,192,256]{2,1,0:T(8,128)S(1)}, u32[]{:S(2)}, u32[]{:S(2)}) collective-permute-start(f32[1,192,256]{2,1,0:T(8,128)S(1)} %get-tuple-element.105), channel_id=1, source_target_pairs={{0,1},{1,2},{2,3},{3,4},{4,5},{5,6},{6,7},{7,8},{8,9},{9,10},{10,1... | collective-permute-start | bytes 589832 | tf_op jit(solution)/shard_map/ppermute | solution.py:22
  2.9 9.3 %copy-start = (bf16[16,192,256]{2,1,0:T(8,128)(2,1)S(1)}, bf16[16,192,256]{2,1,0:T(8,128)(2,1)}, u32[]{:S(2)}) copy-start(bf16[16,192,256]{2,1,0:T(8,128)(2,1)} %param.8) | copy-start | bytes 4718596
  2.9 11.3 %collective-permute-start.1 = (f32[1,192,256]{2,1,0:T(8,128)S(1)}, f32[1,192,256]{2,1,0:T(8,128)S(1)}, u32[]{:S(2)}, u32[]{:S(2)}) collective-permute-start(f32[1,192,256]{2,1,0:T(8,128)S(1)} %get-tuple-element.106), channel_id=1, source_target_pairs={{1,0},{2,1},{3,2},{4,3},{5,4},{6,5},{7,6},{8,7},{9,8},{10,9},{11,1... | collective-permute-start | bytes 589832 | tf_op jit(solution)/shard_map/ppermute | solution.py:24
  12.2 2.1 copy-start.1
  12.2 2.1 copy-start.2
  20.1 7.0 %collective-permute-start.2 = (f32[1,192,256]{2,1,0:T(8,128)S(1)}, f32[1,192,256]{2,1,0:T(8,128)S(1)}, u32[]{:S(2)}, u32[]{:S(2)}) collective-permute-start(f32[1,192,256]{2,1,0:T(8,128)S(1)} %get-tuple-element.101), channel_id=1, source_target_pairs={{0,1},{1,2},{2,3},{3,4},{4,5},{5,6},{6,7},{7,8},{8,9},{9,10},{10,1... | collective-permute-start | bytes 589832 | tf_op jit(solution)/shard_map/ppermute | solution.py:22
  22.1 6.8 %collective-permute-start.3 = (f32[1,192,256]{2,1,0:T(8,128)S(1)}, f32[1,192,256]{2,1,0:T(8,128)S(1)}, u32[]{:S(2)}, u32[]{:S(2)}) collective-permute-start(f32[1,192,256]{2,1,0:T(8,128)S(1)} %get-tuple-element.102), channel_id=1, source_target_pairs={{1,0},{2,1},{3,2},{4,3},{5,4},{6,5},{7,6},{8,7},{9,8},{10,9},{11,1... | collective-permute-start | bytes 589832 | tf_op jit(solution)/shard_map/ppermute | solution.py:24
  32.8 7.2 %copy-start.3 = (s32[48,24]{0,1:T(8,128)S(1)}, s32[48,24]{0,1:T(8,128)}, u32[]{:S(2)}) copy-start(s32[48,24]{0,1:T(8,128)} %param.12) | copy-start | bytes 13828
  32.8 35.2 %all-to-all-start = ((bf16[16,192,256]{2,1,0:T(8,128)(2,1)}), bf16[16,192,256]{2,1,0:T(8,128)(2,1)}, u32[]{:S(2)}, u32[]{:S(2)}) async-start(bf16[16,192,256]{2,1,0:T(8,128)(2,1)} %fusion.27), calls=%async_computation | async-start | bytes 3145728 | tf_op jit(solution)/shard_map/all_to_all | solution.py:97
where the time goes:
time: 265 us; the launch traced here: 263 us
  local copies, waits for them, and re-layouts  105 us (40%)
  matrix products  50.9 us (19%)
  other arithmetic  32.1 us (12%)
  waiting for transfers between devices  29.2 us (11%)
  blocking collectives  26.7 us (10%)
  starting transfers between devices  18.5 us (7%)
    reshape x6, local copies, waits for them, and re-layouts, advance_group(): assembled = assembled.astype(jnp.bfloat16).reshape(group_size * NF, ND * NF)  45 us
    dot_general x6, matrix products, advance_group(): assembled = jnp.einsum('rjc,rjab->racb', selector, weights)  31.6 us
    all_to_all x1, waiting for transfers between devices, local(): lax.all_to_all(moved, 'spec', split_axis=0, concat_axis=1, tiled=True)  27.2 us
    all_to_all x1, blocking collectives, local(): lax.all_to_all(renewed, 'spec', split_axis=1, concat_axis=0, tiled=True)  26.7 us
    dot_general x6, matrix products, advance_group(): jnp.einsum('ak,rkl->ral', assembled, cell_action, preferred_element_type=...  19.2 us
    convert_element_type x1, local copies, waits for them, and re-layouts, source_update(): return result.astype(jnp.bfloat16)  17.5 us
    gather x12, local copies, waits for them, and re-layouts, advance_group(): weights = table[offsets[group_rows]].astype(jnp.float32)  17.1 us
    unnamed x1, other arithmetic  16.6 us
  transfers between devices with their start and end apart: 5, of which 3 were waited for; matrix products, arithmetic and copies ran while one was open for 4% of the time, Pallas kernels for 0%

commit v1 on v0

v1 whole, which is shorter than its diff:
```python
import functools
import math

import jax
import jax.numpy as jnp
from jax import lax
from jax.experimental import pallas as pl
from jax.experimental.pallas import tpu as pltpu
from jax.sharding import PartitionSpec as P

NF = 64
ND = 48
GROUPS = 3
SPEC = 16
TILES = 32
ROWS = 16
LON = 256
HALF = 128
WINDOWS = 8
STRIP = 16
COURANT = 0.45
MESH = pl.DeviceIdType.MESH
BF = jnp.bfloat16
F32 = jnp.float32


def iota(shape, dim):
    return lax.broadcasted_iota(jnp.int32, shape, dim)


def dot(a, b, ca=1, cb=0):
    return lax.dot_general(a, b, (((ca,), (cb,)), ((), ())), preferred_element_type=F32)


def step_kernel(
    action, east, north, mask, pattern, table, out,
    halo, current, coef_e, coef_n, moved, slot_row, window_row, mask_row, onehot, windows, ring,
    send, recv, total, weight, pairs, hits, back_send, back_recv,
    halo_send, halo_recv, cur_send, cur_recv, out_send, out_recv, ret_send, ret_recv,
):
    me = lax.axis_index("spec")
    tile = lax.axis_index("tile")
    up = lax.rem(tile + 1, TILES)
    down = lax.rem(tile + TILES - 1, TILES)

    barrier = pltpu.get_barrier_semaphore()

    def greet(i, carry):
        pl.semaphore_signal(
            barrier, inc=1, device_id={"spec": lax.rem(me + i, SPEC)}, device_id_type=MESH
        )
        return carry

    lax.fori_loop(1, SPEC, greet, 0)
    pl.semaphore_signal(barrier, inc=1, device_id={"tile": up}, device_id_type=MESH)
    pl.semaphore_signal(barrier, inc=1, device_id={"tile": down}, device_id_type=MESH)

    for row in range(ROWS):
        current[row + 1, 0] = jnp.broadcast_to(COURANT * east[row : row + 1, :], (8, LON))
        current[row + 1, 1] = jnp.broadcast_to(COURANT * north[row : row + 1, :], (8, LON))

    pl.semaphore_wait(barrier, SPEC + 1)

    cur_up = pltpu.make_async_remote_copy(
        src_ref=current.at[ROWS], dst_ref=current.at[0],
        send_sem=cur_send.at[0], recv_sem=cur_recv.at[0],
        device_id={"tile": up}, device_id_type=MESH,
    )
    cur_down = pltpu.make_async_remote_copy(
        src_ref=current.at[1], dst_ref=current.at[ROWS + 1],
        send_sem=cur_send.at[1], recv_sem=cur_recv.at[1],
        device_id={"tile": down}, device_id_type=MESH,
    )
    cur_up.start()
    cur_down.start()

    def halo_copies(g):
        comps = pl.ds(pl.multiple_of(g * NF, NF), NF)
        to_up = pltpu.make_async_remote_copy(
            src_ref=action.at[pl.ds(ROWS - 2, 2), comps], dst_ref=halo.at[0, :, comps],
            send_sem=halo_send.at[0, g], recv_sem=halo_recv.at[0, g],
            device_id={"tile": up}, device_id_type=MESH,
        )
        to_down = pltpu.make_async_remote_copy(
            src_ref=action.at[pl.ds(0, 2), comps], dst_ref=halo.at[1, :, comps],
            send_sem=halo_send.at[1, g], recv_sem=halo_recv.at[1, g],
            device_id={"tile": down}, device_id_type=MESH,
        )
        return to_up, to_down

    def start_halo(g, carry):
        to_up, to_down = halo_copies(g)
        to_up.start()
        to_down.start()
        return carry

    lax.fori_loop(0, GROUPS, start_halo, 0)

    speed = jnp.exp(iota((NF, HALF), 0).astype(F32) * (-2.0 / (NF - 1)))
    for g in range(GROUPS):
        direction = jnp.full((8, HALF), me * GROUPS + g, jnp.int32).astype(F32)
        theta = direction * (2.0 * math.pi / ND)
        cosine = COURANT * jnp.cos(theta)
        sine = COURANT * jnp.sin(theta)
        for k in range(0, NF, 8):
            coef_e[g * NF + k : g * NF + k + 8, :] = speed[k : k + 8] * cosine
            coef_n[g * NF + k : g * NF + k + 8, :] = speed[k : k + 8] * sine

    sea = mask[...].astype(F32)
    sea_b = sea.astype(BF)
    before = (iota((LON, LON), 0) <= iota((LON, LON), 1)).astype(F32).astype(BF)
    rank = dot(sea_b, before)
    count = dot(sea_b, jnp.ones((LON, LON), BF))
    lower = (iota((ROWS, ROWS), 1) < iota((ROWS, ROWS), 0)).astype(F32).astype(BF)
    first = dot(lower, count.astype(BF))
    slot = first + rank - 1.0
    slot_mod = slot - LON * jnp.floor(slot * (1.0 / LON))
    place_at = jnp.where(sea > 0.5, slot_mod, -1.0)
    base = jnp.floor(first * (1.0 / LON))
    lane = iota((ROWS, LON), 1).astype(F32)
    window_at = base + jnp.where(lane < first - LON * base, 1.0, 0.0)
    for row in range(ROWS):
        slot_row[row] = place_at[row : row + 1]
        window_row[row] = window_at[row : row + 1]
        mask_row[row] = sea[row : row + 1]

    def build_row(row, carry):
        place = jnp.broadcast_to(slot_row[row], (LON, LON))
        which = iota((LON, LON), 0).astype(F32)
        onehot[row] = jnp.where(place == which, 1.0, 0.0).astype(BF)
        holds = jnp.broadcast_to(window_row[row], (STRIP, LON))
        for w in range(WINDOWS):
            windows[row, w] = jnp.where(holds == float(w), 1.0, 0.0).astype(BF)
        return carry

    lax.fori_loop(0, ROWS, build_row, 0)

    named = pattern[...]
    column = iota((ND, HALF), 1)
    chosen = jnp.zeros((ND, HALF), F32)
    for j in range(ND // 2):
        chosen = chosen + jnp.where(named[:, j : j + 1] == column, 1.0, 0.0)
    chosen = chosen.astype(BF)
    for g in range(GROUPS):
        wide = iota((HALF, SPEC * NF), 1)
        spread = (GROUPS * (wide // NF) + g == iota((HALF, SPEC * NF), 0)).astype(F32).astype(BF)
        wide_hits = dot(chosen, spread)
        for r in range(ND):
            hits[r, :, g * SPEC * NF : (g + 1) * SPEC * NF] = wide_hits[r : r + 1]

    left = (iota((NF, HALF), 0) == iota((NF, HALF), 1)).astype(F32).astype(BF)
    right = (iota((NF, HALF), 0) + NF == iota((NF, HALF), 1)).astype(F32).astype(BF)

    def build_pair(at, carry):
        m = at // SPEC
        s = lax.rem(at, SPEC)
        one = table[GROUPS * s + m]
        two = table[GROUPS * lax.rem(s + 1, SPEC) + m]
        pairs[at] = (dot(one, left) + dot(two, right)).astype(BF)
        return carry

    lax.fori_loop(0, GROUPS * SPEC, build_pair, 0)

    cur_up.wait()
    cur_down.wait()

    keep_south = jnp.where(tile > 0, 1.0, 0.0).astype(F32)
    keep_north = jnp.where(tile < TILES - 1, 1.0, 0.0).astype(F32)

    def propagate(comp):
        comps = pl.ds(comp, STRIP)
        lane_at = iota((STRIP, HALF), 1)
        first_lane = lane_at == 0
        last_lane = lane_at == HALF - 1
        a_e = coef_e[comps, :]
        a_n = coef_n[comps, :]

        def load(row):
            if row < 0:
                whole = halo[0, row + 2, comps, :].astype(F32) * keep_south
            elif row >= ROWS:
                whole = halo[1, row - ROWS, comps, :].astype(F32) * keep_north
            else:
                whole = action[row, comps, :].astype(F32)
            return whole[:, :HALF], whole[:, HALF:]

        def courant(row):
            e = current[row + 1, 0]
            n = current[row + 1, 1]
            res = []
            for h in range(2):
                cols = slice(h * HALF, (h + 1) * HALF)
                ce = a_e + jnp.concatenate([e[:, cols], e[:, cols]], axis=0)
                cn = a_n + jnp.concatenate([n[:, cols], n[:, cols]], axis=0)
                res.append((jnp.abs(ce), ce > 0.0, jnp.abs(cn), cn > 0.0))
            return res

        def update(south, here, north_of, speeds):
            lo, hi = here
            wl, wh = pltpu.roll(lo, 1, 1), pltpu.roll(hi, 1, 1)
            el, eh = pltpu.roll(lo, HALF - 1, 1), pltpu.roll(hi, HALF - 1, 1)
            west = (jnp.where(first_lane, 0.0, wl), jnp.where(first_lane, wl, wh))
            east_of = (jnp.where(last_lane, eh, el), jnp.where(last_lane, 0.0, eh))
            res = []
            for h in range(2):
                size_e, pos_e, size_n, pos_n = speeds[h]
                f = here[h]
                from_e = f - jnp.where(pos_e, west[h], east_of[h])
                from_n = f - jnp.where(pos_n, south[h], north_of[h])
                res.append(f - size_e * from_e - size_n * from_n)
            return tuple(res)

        f0 = {-2: load(-2), -1: load(-1)}
        f1 = {}
        speeds = {}
        for row in range(-1, ROWS + 1):
            f0[row + 1] = load(row + 1)
            speeds[row] = courant(row)
            f1[row] = update(f0[row - 1], f0[row], f0[row + 1], speeds[row])
            if row == -1:
                f1[row] = tuple(x * keep_south for x in f1[row])
            if row == ROWS:
                f1[row] = tuple(x * keep_north for x in f1[row])
            if row >= 1:
                done = update(f1[row - 2], f1[row - 1], f1[row], speeds[row - 1])
                moved[row - 1, comps, :] = jnp.concatenate(done, axis=1).astype(BF)

    def send_copy(g, peer):
        return pltpu.make_async_remote_copy(
            src_ref=send.at[g, peer], dst_ref=recv.at[g, me],
            send_sem=out_send.at[g], recv_sem=out_recv.at[g],
            device_id={"spec": peer}, device_id_type=MESH,
        )

    def back_copy(g, peer):
        return pltpu.make_async_remote_copy(
            src_ref=back_send.at[g, peer], dst_ref=back_recv.at[g, me],
            send_sem=ret_send.at[g], recv_sem=ret_recv.at[g],
            device_id={"spec": peer}, device_id_type=MESH,
        )

    def all_copies(src, dst, send_sem, recv_sem, g):
        others = pl.ds(0, SPEC - 1)
        return pltpu.make_async_remote_copy(
            src_ref=src.at[g, others], dst_ref=dst.at[g, others],
            send_sem=send_sem.at[g], recv_sem=recv_sem.at[g],
            device_id={"spec": lax.rem(me + 1, SPEC)}, device_id_type=MESH,
        )

    def outgoing(g, carry):
        to_up, to_down = halo_copies(g)
        to_up.wait()
        to_down.wait()
        comps = pl.ds(pl.multiple_of(g * NF, NF), NF)

        def strip(s, inner):
            propagate(pl.multiple_of(g * NF + s * STRIP, STRIP))
            return inner

        lax.fori_loop(0, NF // STRIP, strip, 0)

        def squeeze(row, inner):
            ring[row] = dot(moved[row, comps, :], onehot[row], 1, 1).astype(BF)
            return inner

        lax.fori_loop(0, ROWS, squeeze, 0)

        def gather(w, inner):
            for s in range(NF // STRIP):
                rows = slice(s * STRIP, (s + 1) * STRIP)
                packed = jnp.zeros((STRIP, LON), BF)
                for row in range(ROWS):
                    packed = packed + ring[row, rows, :] * windows[row, w]
                send[g, 2 * w, rows, :] = packed[:, :HALF]
                send[g, 2 * w + 1, rows, :] = packed[:, HALF:]
            return inner

        lax.fori_loop(0, WINDOWS, gather, 0)

        def start(i, inner):
            send_copy(g, lax.rem(me + i, SPEC)).start()
            return inner

        lax.fori_loop(1, SPEC, start, 0)
        recv[g, me] = send[g, me]
        return carry

    lax.fori_loop(0, GROUPS, outgoing, 0)

    def build_weight(at, carry):
        g = at // (GROUPS * SPEC)
        h = lax.rem(at // SPEC, GROUPS)
        q = lax.rem(at, SPEC)
        m = lax.rem(g - h + GROUPS, GROUPS)
        carried = (m + h - g) // GROUPS
        for i in range(SPEC // 2):
            s = lax.rem(2 * i - q - carried + 2 * SPEC, SPEC)
            col = pl.multiple_of(g * SPEC * NF + i * HALF, HALF)
            held = hits[GROUPS * q + h, :, pl.ds(col, HALF)]
            held = jnp.broadcast_to(held, (NF, HALF)).astype(BF)
            weight[g * GROUPS + h, pl.ds(pl.multiple_of(q * NF, NF), NF), i * HALF : (i + 1) * HALF] = (
                pairs[m * SPEC + s] * held
            )
        return carry

    lax.fori_loop(0, GROUPS * GROUPS * SPEC, build_weight, 0)

    for g in range(GROUPS):
        all_copies(send, recv, out_send, out_recv, g).wait_recv()

        def couple(h, carry, g=g):
            cells = recv[g].reshape(SPEC * NF, HALF)
            part = dot(weight[g * GROUPS + h], cells)
            if g == 0:
                total[h] = part
            elif g < GROUPS - 1:
                total[h] = total[h] + part
            else:
                coupled = total[h] + part
                own = recv[h].reshape(SPEC * NF, HALF).astype(F32)
                renewed = (own + own * coupled).astype(BF)
                back_send[h] = renewed.reshape(SPEC, NF, HALF)

                def start(i, inner):
                    back_copy(h, lax.rem(me + i, SPEC)).start()
                    return inner

                lax.fori_loop(1, SPEC, start, 0)
                back_recv[h, me] = back_send[h, me]
            return carry

        lax.fori_loop(0, GROUPS, couple, 0)

    def incoming(h, carry):
        all_copies(back_send, back_recv, ret_send, ret_recv, h).wait_recv()
        comps = pl.ds(pl.multiple_of(h * NF, NF), NF)

        def spread(row, inner):
            for s in range(NF // STRIP):
                rows = slice(s * STRIP, (s + 1) * STRIP)
                for half in range(2):
                    cols = slice(half * HALF, (half + 1) * HALF)
                    picked = jnp.zeros((STRIP, HALF), BF)
                    for w in range(WINDOWS):
                        picked = picked + back_recv[h, 2 * w + half, rows, :] * windows[row, w, :, cols]
                    ring[row, rows, cols] = picked
            wide = dot(ring[row], onehot[row], 1, 0)
            at_sea = jnp.broadcast_to(mask_row[row], (NF, LON)) > 0.5
            result = jnp.where(at_sea, wide, moved[row, comps, :].astype(F32))
            out[row, comps, :] = result.astype(BF)
            return inner

        lax.fori_loop(0, ROWS, spread, 0)
        return carry

    lax.fori_loop(0, GROUPS, incoming, 0)

    def finish(g, carry):
        all_copies(send, recv, out_send, out_recv, g).wait_send()
        all_copies(back_send, back_recv, ret_send, ret_recv, g).wait_send()
        return carry

    lax.fori_loop(0, GROUPS, finish, 0)


def local(action, east_current, north_current, sea_mask, pattern, table):
    vmem = pl.BlockSpec(memory_space=pltpu.VMEM)
    dma = pltpu.SemaphoreType.DMA
    comps = GROUPS * NF
    return pl.pallas_call(
        step_kernel,
        out_shape=jax.ShapeDtypeStruct((ROWS, comps, LON), BF),
        in_specs=[vmem] * 6,
        out_specs=vmem,
        scratch_shapes=[
            pltpu.VMEM((2, 2, comps, LON), BF),
            pltpu.VMEM((ROWS + 2, 2, 8, LON), F32),
            pltpu.VMEM((comps, HALF), F32),
            pltpu.VMEM((comps, HALF), F32),
            pltpu.VMEM((ROWS, comps, LON), BF),
            pltpu.VMEM((ROWS, 1, LON), F32),
            pltpu.VMEM((ROWS, 1, LON), F32),
            pltpu.VMEM((ROWS, 1, LON), F32),
            pltpu.VMEM((ROWS, LON, LON), BF),
            pltpu.VMEM((ROWS, WINDOWS, STRIP, LON), BF),
            pltpu.VMEM((ROWS, NF, LON), BF),
            pltpu.VMEM((GROUPS, SPEC, NF, HALF), BF),
            pltpu.VMEM((GROUPS, SPEC, NF, HALF), BF),
            pltpu.VMEM((GROUPS, SPEC * NF, HALF), F32),
            pltpu.VMEM((GROUPS * GROUPS, SPEC * NF, SPEC * NF), BF),
            pltpu.VMEM((GROUPS * SPEC, NF, HALF), BF),
            pltpu.VMEM((ND, 1, ND * NF), F32),
            pltpu.VMEM((GROUPS, SPEC, NF, HALF), BF),
            pltpu.VMEM((GROUPS, SPEC, NF, HALF), BF),
            dma((2, GROUPS)),
            dma((2, GROUPS)),
            dma((2,)),
            dma((2,)),
            dma((GROUPS,)),
            dma((GROUPS,)),
            dma((GROUPS,)),
            dma((GROUPS,)),
        ],
        compiler_params=pltpu.CompilerParams(
            collective_id=0, has_side_effects=True, vmem_limit_bytes=52 * 1024 * 1024
        ),
    )(action, east_current, north_current, sea_mask, pattern, table)


def solution(mesh):
    return jax.shard_map(
        local,
        mesh=mesh,
        in_specs=(
            P("tile", "spec", None),
            P("tile", None),
            P("tile", None),
            P("tile", None),
            P(),
            P(),
        ),
        out_specs=P("tile", "spec", None),
        check_vma=False,
    )
```

time: 265 us -> 75.8 us (0.29)
  the two profiles are of different devices: /device:TPU:416 before, /device:TPU:2 now
where the time goes in v1:
time: 75.8 us; the launch traced here: 75.3 us
  Pallas kernels  68.6 us (91%)
  local copies, waits for them, and re-layouts  6.76 us (9%)
    pallas_call x1, Pallas kernels, local(): pl.pallas_call(step_kernel, out_shape=jax.ShapeDtypeStruct((ROWS, comps,...  68.6 us
    unnamed x10, local copies, waits for them, and re-layouts  6.76 us

profile of v1, /device:TPU:2, one launch (start us, length us, event | category | flops | bytes accessed | tf_op | source)
XLA Modules:
  0.0 75.3 jit_solution(11901481324184899367)
XLA Ops:
  0.0 0.8 %copy.7.pattern = s32[48,24]{1,0:T(8,128)S(1)} copy(s32[48,24]{0,1:T(8,128)} %param.10) | data formatting | bytes 9216 | tf_op args[4]
  0.8 0.0 copy-start
  0.8 1.1 %copy-done = bf16[48,64,64]{2,1,0:T(8,128)(2,1)S(1)} copy-done((bf16[48,64,64]{2,1,0:T(8,128)(2,1)S(1)}, bf16[48,64,64]{2,1,0:T(8,128)(2,1)}, u32[]{:S(2)}) %copy-start) | copy-done | bytes 393240
  1.9 0.0 copy-start.1
  1.9 0.7 copy-done.1
  2.6 0.0 copy-start.2
  2.6 0.7 copy-done.2
  3.4 0.0 copy-start.3
  3.4 0.7 copy-done.3
  4.1 68.6 %shard_map.64 = bf16[16,192,256]{2,1,0:T(8,128)(2,1)} custom-call(bf16[16,192,256]{2,1,0:T(8,128)(2,1)} %action.1, f32[16,256]{1,0:T(8,128)S(1)} %copy-done.1, f32[16,256]{1,0:T(8,128)S(1)} %copy-done.2, s32[16,256]{1,0:T(8,128)S(1)} %copy-done.3, s32[48,24]{1,0:T(8,128)S(1)} %copy.7.pattern, bf16[48,64,64]{2,1,0:T(8,128)(2,1)S(1)} %copy-done), custom_call_target="tpu_custom_call" | custom-call | tf_op jit(solution)/shard_map/pallas_call | solution.py:370
  72.6 2.7 %copy.9 = bf16[16,192,256]{2,1,0:T(8,128)(2,1)} copy(bf16[16,192,256]{2,1,0:T(8,128)(2,1)} %shard_map.64) | data formatting | bytes 3145728
Async XLA Ops:
  0.8 1.1 %copy-start = (bf16[48,64,64]{2,1,0:T(8,128)(2,1)S(1)}, bf16[48,64,64]{2,1,0:T(8,128)(2,1)}, u32[]{:S(2)}) copy-start(bf16[48,64,64]{2,1,0:T(8,128)(2,1)} %table.1) | copy-start | bytes 1179652
  1.9 0.7 copy-start.1
  2.6 0.7 copy-start.2
  3.4 0.7 copy-start.3

commit v2 on v1

--- a/solution.py
+++ b/solution.py
@@ -33,16 +33,37 @@
 
 
 def step_kernel(
-    action, east, north, mask, pattern, table, out,
-    halo, current, coef_e, coef_n, moved, slot_row, window_row, mask_row, onehot, windows, ring,
+    action_hbm, east_hbm, north_hbm, mask_hbm, pattern_hbm, table_hbm, out_hbm, moved_hbm,
+    action, east, north, mask, pattern, table, out, halo, current, coef_e, coef_n, moved, slot_row, window_row, onehot, windows, ring,
     send, recv, total, weight, pairs, hits, back_send, back_recv,
     halo_send, halo_recv, cur_send, cur_recv, out_send, out_recv, ret_send, ret_recv,
+    load_sem, action_sem, store_sem, moved_sem,
 ):
     me = lax.axis_index("spec")
     tile = lax.axis_index("tile")
     up = lax.rem(tile + 1, TILES)
     down = lax.rem(tile + TILES - 1, TILES)
 
+    small = [
+        pltpu.make_async_copy(src, dst, load_sem.at[i])
+        for i, (src, dst) in enumerate(
+            ((east_hbm, east), (north_hbm, north), (mask_hbm, mask), (pattern_hbm, pattern), (table_hbm, table))
+        )
+    ]
+    for copy in small:
+        copy.start()
+
+    def group(g):
+        return pl.ds(pl.multiple_of(g * NF, NF), NF)
+
+    def action_copy(g):
+        return pltpu.make_async_copy(
+            action_hbm.at[:, group(g)], action.at[:, group(g)], action_sem.at[g]
+        )
+
+    for g in range(GROUPS):
+        action_copy(g).start()
+
     barrier = pltpu.get_barrier_semaphore()
 
     def greet(i, carry):
@@ -54,6 +75,9 @@
     lax.fori_loop(1, SPEC, greet, 0)
     pl.semaphore_signal(barrier, inc=1, device_id={"tile": up}, device_id_type=MESH)
     pl.semaphore_signal(barrier, inc=1, device_id={"tile": down}, device_id_type=MESH)
+
+    small[0].wait()
+    small[1].wait()
 
     for row in range(ROWS):
         current[row + 1, 0] = jnp.broadcast_to(COURANT * east[row : row + 1, :], (8, LON))
@@ -75,14 +99,14 @@
     cur_down.start()
 
     def halo_copies(g):
-        comps = pl.ds(pl.multiple_of(g * NF, NF), NF)
+        comps = group(g)
         to_up = pltpu.make_async_remote_copy(
-            src_ref=action.at[pl.ds(ROWS - 2, 2), comps], dst_ref=halo.at[0, :, comps],
+            src_ref=action_hbm.at[pl.ds(ROWS - 2, 2), comps], dst_ref=halo.at[0, :, comps],
             send_sem=halo_send.at[0, g], recv_sem=halo_recv.at[0, g],
             device_id={"tile": up}, device_id_type=MESH,
         )
         to_down = pltpu.make_async_remote_copy(
-            src_ref=action.at[pl.ds(0, 2), comps], dst_ref=halo.at[1, :, comps],
+            src_ref=action_hbm.at[pl.ds(0, 2), comps], dst_ref=halo.at[1, :, comps],
             send_sem=halo_send.at[1, g], recv_sem=halo_recv.at[1, g],
             device_id={"tile": down}, device_id_type=MESH,
         )
@@ -106,6 +130,7 @@
             coef_e[g * NF + k : g * NF + k + 8, :] = speed[k : k + 8] * cosine
             coef_n[g * NF + k : g * NF + k + 8, :] = speed[k : k + 8] * sine
 
+    small[2].wait()
     sea = mask[...].astype(F32)
     sea_b = sea.astype(BF)
     before = (iota((LON, LON), 0) <= iota((LON, LON), 1)).astype(F32).astype(BF)
@@ -122,7 +147,6 @@
     for row in range(ROWS):
         slot_row[row] = place_at[row : row + 1]
         window_row[row] = window_at[row : row + 1]
-        mask_row[row] = sea[row : row + 1]
 
     def build_row(row, carry):
         place = jnp.broadcast_to(slot_row[row], (LON, LON))
@@ -135,31 +159,32 @@
 
     lax.fori_loop(0, ROWS, build_row, 0)
 
-    named = pattern[...]
-    column = iota((ND, HALF), 1)
-    chosen = jnp.zeros((ND, HALF), F32)
+    small[3].wait()
+    column = iota((HALF, ND), 0)
+    chosen = jnp.zeros((HALF, ND), F32)
     for j in range(ND // 2):
-        chosen = chosen + jnp.where(named[:, j : j + 1] == column, 1.0, 0.0)
+        named = jnp.broadcast_to(pattern[j : j + 1, :], (HALF, ND))
+        chosen = chosen + jnp.where(named == column, 1.0, 0.0)
     chosen = chosen.astype(BF)
     for g in range(GROUPS):
         wide = iota((HALF, SPEC * NF), 1)
         spread = (GROUPS * (wide // NF) + g == iota((HALF, SPEC * NF), 0)).astype(F32).astype(BF)
-        wide_hits = dot(chosen, spread)
+        wide_hits = dot(chosen, spread, 0, 0)
         for r in range(ND):
             hits[r, :, g * SPEC * NF : (g + 1) * SPEC * NF] = wide_hits[r : r + 1]
 
-    left = (iota((NF, HALF), 0) == iota((NF, HALF), 1)).astype(F32).astype(BF)
-    right = (iota((NF, HALF), 0) + NF == iota((NF, HALF), 1)).astype(F32).astype(BF)
-
-    def build_pair(at, carry):
-        m = at // SPEC
-        s = lax.rem(at, SPEC)
-        one = table[GROUPS * s + m]
-        two = table[GROUPS * lax.rem(s + 1, SPEC) + m]
-        pairs[at] = (dot(one, left) + dot(two, right)).astype(BF)
-        return carry
-
-    lax.fori_loop(0, GROUPS * SPEC, build_pair, 0)
+    small[4].wait()
+
+    def build_pair(s, carry):
+        for m in range(GROUPS):
+            one = table[GROUPS * s + m]
+            two = table[GROUPS * lax.rem(s + 1, SPEC) + m]
+            pair = jnp.concatenate([one, two], axis=1)
+            pairs[m * 2 * SPEC + s] = pair
+            pairs[m * 2 * SPEC + SPEC + s] = pair
+        return carry
+
+    lax.fori_loop(0, SPEC, build_pair, 0)
 
     cur_up.wait()
     cur_down.wait()
@@ -225,6 +250,11 @@
                 done = update(f1[row - 2], f1[row - 1], f1[row], speeds[row - 1])
                 moved[row - 1, comps, :] = jnp.concatenate(done, axis=1).astype(BF)
 
+    def moved_copy(g):
+        return pltpu.make_async_copy(
+            moved.at[:, group(g)], moved_hbm.at[:, group(g)], moved_sem.at[g]
+        )
+
     def send_copy(g, peer):
         return pltpu.make_async_remote_copy(
             src_ref=send.at[g, peer], dst_ref=recv.at[g, me],
@@ -249,9 +279,10 @@
 
     def outgoing(g, carry):
         to_up, to_down = halo_copies(g)
+        action_copy(g).wait()
         to_up.wait()
         to_down.wait()
-        comps = pl.ds(pl.multiple_of(g * NF, NF), NF)
+        comps = group(g)
 
         def strip(s, inner):
             propagate(pl.multiple_of(g * NF + s * STRIP, STRIP))
@@ -259,11 +290,9 @@
 
         lax.fori_loop(0, NF // STRIP, strip, 0)
 
-        def squeeze(row, inner):
+        moved_copy(g).start()
+        for row in range(ROWS):
             ring[row] = dot(moved[row, comps, :], onehot[row], 1, 1).astype(BF)
-            return inner
-
-        lax.fori_loop(0, ROWS, squeeze, 0)
 
         def gather(w, inner):
             for s in range(NF // STRIP):
@@ -287,23 +316,26 @@
 
     lax.fori_loop(0, GROUPS, outgoing, 0)
 
-    def build_weight(at, carry):
-        g = at // (GROUPS * SPEC)
-        h = lax.rem(at // SPEC, GROUPS)
-        q = lax.rem(at, SPEC)
-        m = lax.rem(g - h + GROUPS, GROUPS)
-        carried = (m + h - g) // GROUPS
-        for i in range(SPEC // 2):
-            s = lax.rem(2 * i - q - carried + 2 * SPEC, SPEC)
-            col = pl.multiple_of(g * SPEC * NF + i * HALF, HALF)
-            held = hits[GROUPS * q + h, :, pl.ds(col, HALF)]
-            held = jnp.broadcast_to(held, (NF, HALF)).astype(BF)
-            weight[g * GROUPS + h, pl.ds(pl.multiple_of(q * NF, NF), NF), i * HALF : (i + 1) * HALF] = (
-                pairs[m * SPEC + s] * held
-            )
-        return carry
-
-    lax.fori_loop(0, GROUPS * GROUPS * SPEC, build_weight, 0)
+    for g in range(GROUPS):
+        for h in range(GROUPS):
+            m = (g - h) % GROUPS
+            carried = (m + h - g) // GROUPS
+
+            def build_weight(q, carry, g=g, h=h, m=m, carried=carried):
+                at = m * 2 * SPEC + SPEC - carried - q
+                for i in range(SPEC // 2):
+                    col = g * SPEC * NF + i * HALF
+                    held = hits[GROUPS * q + h, :, col : col + HALF]
+                    held = jnp.broadcast_to(held, (STRIP, HALF)).astype(BF)
+                    for k in range(0, NF, STRIP):
+                        weight[
+                            g * GROUPS + h,
+                            pl.ds(pl.multiple_of(q * NF + k, STRIP), STRIP),
+                            i * HALF : (i + 1) * HALF,
+                        ] = pairs[at + 2 * i, k : k + STRIP, :] * held
+                return carry
+
+            lax.fori_loop(0, SPEC, build_weight, 0)
 
     for g in range(GROUPS):
         all_copies(send, recv, out_send, out_recv, g).wait_recv()
@@ -331,11 +363,14 @@
 
         lax.fori_loop(0, GROUPS, couple, 0)
 
+    def out_copy(h):
+        return pltpu.make_async_copy(out.at[:, group(h)], out_hbm.at[:, group(h)], store_sem.at[h])
+
     def incoming(h, carry):
         all_copies(back_send, back_recv, ret_send, ret_recv, h).wait_recv()
-        comps = pl.ds(pl.multiple_of(h * NF, NF), NF)
-
-        def spread(row, inner):
+        comps = group(h)
+
+        def pick(row, inner):
             for s in range(NF // STRIP):
                 rows = slice(s * STRIP, (s + 1) * STRIP)
                 for half in range(2):
@@ -344,13 +379,12 @@
                     for w in range(WINDOWS):
                         picked = picked + back_recv[h, 2 * w + half, rows, :] * windows[row, w, :, cols]
                     ring[row, rows, cols] = picked
-            wide = dot(ring[row], onehot[row], 1, 0)
-            at_sea = jnp.broadcast_to(mask_row[row], (NF, LON)) > 0.5
-            result = jnp.where(at_sea, wide, moved[row, comps, :].astype(F32))
-            out[row, comps, :] = result.astype(BF)
             return inner
 
-        lax.fori_loop(0, ROWS, spread, 0)
+        lax.fori_loop(0, ROWS, pick, 0)
+        for row in range(ROWS):
+            out[row, comps, :] = dot(ring[row], onehot[row], 1, 0).astype(BF)
+        out_copy(h).start()
         return carry
 
     lax.fori_loop(0, GROUPS, incoming, 0)
@@ -358,27 +392,35 @@
     def finish(g, carry):
         all_copies(send, recv, out_send, out_recv, g).wait_send()
         all_copies(back_send, back_recv, ret_send, ret_recv, g).wait_send()
+        out_copy(g).wait()
+        moved_copy(g).wait()
         return carry
 
     lax.fori_loop(0, GROUPS, finish, 0)
 
 
 def local(action, east_current, north_current, sea_mask, pattern, table):
-    vmem = pl.BlockSpec(memory_space=pltpu.VMEM)
+    hbm = pl.BlockSpec(memory_space=pltpu.HBM)
     dma = pltpu.SemaphoreType.DMA
     comps = GROUPS * NF
-    return pl.pallas_call(
+    renewed, moved = pl.pallas_call(
         step_kernel,
-        out_shape=jax.ShapeDtypeStruct((ROWS, comps, LON), BF),
-        in_specs=[vmem] * 6,
-        out_specs=vmem,
+        out_shape=[jax.ShapeDtypeStruct((ROWS, comps, LON), BF)] * 2,
+        in_specs=[hbm] * 6,
+        out_specs=[hbm] * 2,
         scratch_shapes=[
+            pltpu.VMEM((ROWS, comps, LON), BF),
+            pltpu.VMEM((ROWS, LON), F32),
+            pltpu.VMEM((ROWS, LON), F32),
+            pltpu.VMEM((ROWS, LON), jnp.int32),
+            pltpu.VMEM((ND // 2, ND), jnp.int32),
+            pltpu.VMEM((ND, NF, NF), BF),
+            pltpu.VMEM((ROWS, comps, LON), BF),
             pltpu.VMEM((2, 2, comps, LON), BF),
             pltpu.VMEM((ROWS + 2, 2, 8, LON), F32),
             pltpu.VMEM((comps, HALF), F32),
             pltpu.VMEM((comps, HALF), F32),
             pltpu.VMEM((ROWS, comps, LON), BF),
-            pltpu.VMEM((ROWS, 1, LON), F32),
             pltpu.VMEM((ROWS, 1, LON), F32),
             pltpu.VMEM((ROWS, 1, LON), F32),
             pltpu.VMEM((ROWS, LON, LON), BF),
@@ -388,7 +430,7 @@
             pltpu.VMEM((GROUPS, SPEC, NF, HALF), BF),
             pltpu.VMEM((GROUPS, SPEC * NF, HALF), F32),
             pltpu.VMEM((GROUPS * GROUPS, SPEC * NF, SPEC * NF), BF),
-            pltpu.VMEM((GROUPS * SPEC, NF, HALF), BF),
+            pltpu.VMEM((GROUPS * 2 * SPEC, NF, HALF), BF),
             pltpu.VMEM((ND, 1, ND * NF), F32),
             pltpu.VMEM((GROUPS, SPEC, NF, HALF), BF),
             pltpu.VMEM((GROUPS, SPEC, NF, HALF), BF),
@@ -400,11 +442,16 @@
             dma((GROUPS,)),
             dma((GROUPS,)),
             dma((GROUPS,)),
+            dma((5,)),
+            dma((GROUPS,)),
+            dma((GROUPS,)),
+            dma((GROUPS,)),
         ],
         compiler_params=pltpu.CompilerParams(
-            collective_id=0, has_side_effects=True, vmem_limit_bytes=52 * 1024 * 1024
+            collective_id=0, has_side_effects=True, vmem_limit_bytes=64 * 1024 * 1024
         ),
-    )(action, east_current, north_current, sea_mask, pattern, table)
+    )(action, east_current, north_current, sea_mask, pattern.T, table)
+    return jnp.where(sea_mask[:, None, :] > 0, renewed, moved)
 
 
 def solution(mesh):

time: 75.8 us -> 51.9 us (0.68)
  the two profiles are of different devices: /device:TPU:2 before, /device:TPU:8 now
where the time goes in v2:
time: 51.9 us; the launch traced here: 51.7 us
  Pallas kernels  47.2 us (91%)
  other arithmetic  4.5 us (9%)
    pallas_call x1, Pallas kernels, local(): pl.pallas_call(step_kernel, out_shape=[jax.ShapeDtypeStruct((ROWS, comps,...  47.2 us
    select_n x1, other arithmetic, local(): return jnp.where(sea_mask[:, None, :] > 0, renewed, moved)  3.19 us
    gt x1, other arithmetic, local(): return jnp.where(sea_mask[:, None, :] > 0, renewed, moved)  1.3 us

profile of v2, /device:TPU:8, one launch (start us, length us, event | category | flops | bytes accessed | tf_op | source)
XLA Modules:
  0.0 51.7 jit_solution(5878116215630186938)
XLA Ops:
  0.0 1.3 %broadcast_compare_fusion = pred[16,256]{1,0:T(8,128)(4,1)} fusion(s32[16,256]{1,0:T(8,128)} %mask_hbm.1), kind=kLoop, calls=%fused_computation.1 | loop fusion | flops 4096 | bytes 20480 | tf_op jit(solution)/shard_map/gt | solution.py:454
  1.3 47.2 %shard_map.64 = (bf16[16,192,256]{2,1,0:T(8,128)(2,1)}, bf16[16,192,256]{2,1,0:T(8,128)(2,1)}) custom-call(bf16[16,192,256]{2,1,0:T(8,128)(2,1)} %action_hbm.1, f32[16,256]{1,0:T(8,128)} %east_hbm.1, f32[16,256]{1,0:T(8,128)} %north_hbm.1, s32[16,256]{1,0:T(8,128)} %mask_hbm.1, s32[24,48]{1,0:T(8,128)} %bitcast.1, bf16[48,64,64]{2,1,0:T(8,128)(2,1)} %table_hbm.1), custom_call_target="tpu_custom_call" | custom-call | tf_op jit(solution)/shard_map/pallas_call | solution.py:406
  48.5 3.2 %broadcast_select_fusion = bf16[16,192,256]{2,1,0:T(8,128)(2,1)} fusion(bf16[16,192,256]{2,1,0:T(8,128)(2,1)} %get-tuple-element.7, bf16[16,192,256]{2,1,0:T(8,128)(2,1)} %get-tuple-element.8, pred[16,256]{1,0:T(8,128)(4,1)} %broadcast_compare_fusion), kind=kLoop, calls=%fused_computation | loop fusion | flops 786432 | bytes 4722688 | tf_op jit(solution)/shard_map/jit(_where)/select_n | solution.py:454

commit v3 on v2

--- a/solution.py
+++ b/solution.py
@@ -33,17 +33,31 @@
 
 
 def step_kernel(
-    action_hbm, east_hbm, north_hbm, mask_hbm, pattern_hbm, table_hbm, out_hbm, moved_hbm,
-    action, east, north, mask, pattern, table, out, halo, current, coef_e, coef_n, moved, slot_row, window_row, onehot, windows, ring,
-    send, recv, total, weight, pairs, hits, back_send, back_recv,
+    action_hbm, east_hbm, north_hbm, mask_hbm, pattern_hbm, table_hbm, out_hbm,
+    action, east, north, mask, pattern, table, out, halo, current, coef_e, coef_n, moved, slot_row, window_row, mask_row, onehot, windows, ring,
+    send, recv, total, weight_a, weight_b, pairs, hits, back_send, back_recv,
     halo_send, halo_recv, cur_send, cur_recv, out_send, out_recv, ret_send, ret_recv,
-    load_sem, action_sem, store_sem, moved_sem,
+    load_sem, action_sem, store_sem,
 ):
+    weight = (weight_a, weight_b)
     me = lax.axis_index("spec")
     tile = lax.axis_index("tile")
     up = lax.rem(tile + 1, TILES)
     down = lax.rem(tile + TILES - 1, TILES)
 
+    barrier = pltpu.get_barrier_semaphore()
+
+    pl.semaphore_signal(barrier, inc=1, device_id={"tile": up}, device_id_type=MESH)
+    pl.semaphore_signal(barrier, inc=1, device_id={"tile": down}, device_id_type=MESH)
+
+    def greet(i, carry):
+        pl.semaphore_signal(
+            barrier, inc=1, device_id={"spec": lax.rem(me + i, SPEC)}, device_id_type=MESH
+        )
+        return carry
+
+    lax.fori_loop(1, SPEC, greet, 0)
+
     small = [
         pltpu.make_async_copy(src, dst, load_sem.at[i])
         for i, (src, dst) in enumerate(
@@ -64,17 +78,6 @@
     for g in range(GROUPS):
         action_copy(g).start()
 
-    barrier = pltpu.get_barrier_semaphore()
-
-    def greet(i, carry):
-        pl.semaphore_signal(
-            barrier, inc=1, device_id={"spec": lax.rem(me + i, SPEC)}, device_id_type=MESH
-        )
-        return carry
-
-    lax.fori_loop(1, SPEC, greet, 0)
-    pl.semaphore_signal(barrier, inc=1, device_id={"tile": up}, device_id_type=MESH)
-    pl.semaphore_signal(barrier, inc=1, device_id={"tile": down}, device_id_type=MESH)
 
     small[0].wait()
     small[1].wait()
@@ -147,6 +150,7 @@
     for row in range(ROWS):
         slot_row[row] = place_at[row : row + 1]
         window_row[row] = window_at[row : row + 1]
+        mask_row[row] = sea[row : row + 1]
 
     def build_row(row, carry):
         place = jnp.broadcast_to(slot_row[row], (LON, LON))
@@ -202,12 +206,15 @@
 
         def load(row):
             if row < 0:
-                whole = halo[0, row + 2, comps, :].astype(F32) * keep_south
+                whole = halo[0, row + 2, comps, :] * keep_south.astype(BF)
             elif row >= ROWS:
-                whole = halo[1, row - ROWS, comps, :].astype(F32) * keep_north
+                whole = halo[1, row - ROWS, comps, :] * keep_north.astype(BF)
             else:
-                whole = action[row, comps, :].astype(F32)
+                whole = action[row, comps, :]
             return whole[:, :HALF], whole[:, HALF:]
+
+        def wide(pair):
+            return tuple(x.astype(F32) for x in pair)
 
         def courant(row):
             e = current[row + 1, 0]
@@ -220,10 +227,12 @@
                 res.append((jnp.abs(ce), ce > 0.0, jnp.abs(cn), cn > 0.0))
             return res
 
-        def update(south, here, north_of, speeds):
-            lo, hi = here
-            wl, wh = pltpu.roll(lo, 1, 1), pltpu.roll(hi, 1, 1)
-            el, eh = pltpu.roll(lo, HALF - 1, 1), pltpu.roll(hi, HALF - 1, 1)
+        def turn(pair, shift):
+            return tuple(pltpu.roll(x, shift, 1).astype(F32) for x in pair)
+
+        def update(south, here, north_of, speeds, narrow=None):
+            wl, wh = turn(narrow or here, 1)
+            el, eh = turn(narrow or here, HALF - 1)
             west = (jnp.where(first_lane, 0.0, wl), jnp.where(first_lane, wl, wh))
             east_of = (jnp.where(last_lane, eh, el), jnp.where(last_lane, 0.0, eh))
             res = []
@@ -235,13 +244,15 @@
                 res.append(f - size_e * from_e - size_n * from_n)
             return tuple(res)
 
-        f0 = {-2: load(-2), -1: load(-1)}
+        raw = {-2: load(-2), -1: load(-1)}
+        f0 = {-2: wide(raw[-2]), -1: wide(raw[-1])}
         f1 = {}
         speeds = {}
         for row in range(-1, ROWS + 1):
-            f0[row + 1] = load(row + 1)
+            raw[row + 1] = load(row + 1)
+            f0[row + 1] = wide(raw[row + 1])
             speeds[row] = courant(row)
-            f1[row] = update(f0[row - 1], f0[row], f0[row + 1], speeds[row])
+            f1[row] = update(f0[row - 1], f0[row], f0[row + 1], speeds[row], raw[row])
             if row == -1:
                 f1[row] = tuple(x * keep_south for x in f1[row])
             if row == ROWS:
@@ -250,11 +261,6 @@
                 done = update(f1[row - 2], f1[row - 1], f1[row], speeds[row - 1])
                 moved[row - 1, comps, :] = jnp.concatenate(done, axis=1).astype(BF)
 
-    def moved_copy(g):
-        return pltpu.make_async_copy(
-            moved.at[:, group(g)], moved_hbm.at[:, group(g)], moved_sem.at[g]
-        )
-
     def send_copy(g, peer):
         return pltpu.make_async_remote_copy(
             src_ref=send.at[g, peer], dst_ref=recv.at[g, me],
@@ -277,7 +283,7 @@
             device_id={"spec": lax.rem(me + 1, SPEC)}, device_id_type=MESH,
         )
 
-    def outgoing(g, carry):
+    def outgoing(g):
         to_up, to_down = halo_copies(g)
         action_copy(g).wait()
         to_up.wait()
@@ -290,7 +296,6 @@
 
         lax.fori_loop(0, NF // STRIP, strip, 0)
 
-        moved_copy(g).start()
         for row in range(ROWS):
             ring[row] = dot(moved[row, comps, :], onehot[row], 1, 1).astype(BF)
 
@@ -312,37 +317,29 @@
 
         lax.fori_loop(1, SPEC, start, 0)
         recv[g, me] = send[g, me]
-        return carry
-
-    lax.fori_loop(0, GROUPS, outgoing, 0)
-
-    for g in range(GROUPS):
+
+    def build_weight(at, q):
+        g, h = divmod(at, GROUPS)
+        m = (g - h) % GROUPS
+        first_pair = m * 2 * SPEC + SPEC - (m + h - g) // GROUPS - q
+        for i in range(SPEC // 2):
+            col = g * SPEC * NF + i * HALF
+            held = hits[GROUPS * q + h, :, col : col + HALF]
+            held = jnp.broadcast_to(held, (STRIP, HALF)).astype(BF)
+            for k in range(0, NF, STRIP):
+                weight[at % 2][q * NF + k : q * NF + k + STRIP, i * HALF : (i + 1) * HALF] = (
+                    pairs[first_pair + 2 * i, k : k + STRIP, :] * held
+                )
+
+    def couple(g):
+        all_copies(send, recv, out_send, out_recv, g).wait_recv()
+        cells = recv[g].reshape(SPEC * NF, HALF)
         for h in range(GROUPS):
-            m = (g - h) % GROUPS
-            carried = (m + h - g) // GROUPS
-
-            def build_weight(q, carry, g=g, h=h, m=m, carried=carried):
-                at = m * 2 * SPEC + SPEC - carried - q
-                for i in range(SPEC // 2):
-                    col = g * SPEC * NF + i * HALF
-                    held = hits[GROUPS * q + h, :, col : col + HALF]
-                    held = jnp.broadcast_to(held, (STRIP, HALF)).astype(BF)
-                    for k in range(0, NF, STRIP):
-                        weight[
-                            g * GROUPS + h,
-                            pl.ds(pl.multiple_of(q * NF + k, STRIP), STRIP),
-                            i * HALF : (i + 1) * HALF,
-                        ] = pairs[at + 2 * i, k : k + STRIP, :] * held
-                return carry
-
-            lax.fori_loop(0, SPEC, build_weight, 0)
-
-    for g in range(GROUPS):
-        all_copies(send, recv, out_send, out_recv, g).wait_recv()
-
-        def couple(h, carry, g=g):
-            cells = recv[g].reshape(SPEC * NF, HALF)
-            part = dot(weight[g * GROUPS + h], cells)
+            at = g * GROUPS + h
+            part = dot(weight[at % 2][...], cells)
+            if at + 1 < GROUPS * GROUPS:
+                for q in range(SPEC):
+                    build_weight(at + 1, q)
             if g == 0:
                 total[h] = part
             elif g < GROUPS - 1:
@@ -353,15 +350,21 @@
                 renewed = (own + own * coupled).astype(BF)
                 back_send[h] = renewed.reshape(SPEC, NF, HALF)
 
-                def start(i, inner):
+                def start(i, inner, h=h):
                     back_copy(h, lax.rem(me + i, SPEC)).start()
                     return inner
 
                 lax.fori_loop(1, SPEC, start, 0)
                 back_recv[h, me] = back_send[h, me]
-            return carry
-
-        lax.fori_loop(0, GROUPS, couple, 0)
+
+    for q in range(SPEC):
+        build_weight(0, q)
+    outgoing(0)
+    outgoing(1)
+    couple(0)
+    outgoing(2)
+    couple(1)
+    couple(2)
 
     def out_copy(h):
         return pltpu.make_async_copy(out.at[:, group(h)], out_hbm.at[:, group(h)], store_sem.at[h])
@@ -383,7 +386,10 @@
 
         lax.fori_loop(0, ROWS, pick, 0)
         for row in range(ROWS):
-            out[row, comps, :] = dot(ring[row], onehot[row], 1, 0).astype(BF)
+            wide = dot(ring[row], onehot[row], 1, 0)
+            at_sea = jnp.broadcast_to(mask_row[row], (NF, LON)) > 0.5
+            result = jnp.where(at_sea, wide, moved[row, comps, :].astype(F32))
+            out[row, comps, :] = result.astype(BF)
         out_copy(h).start()
         return carry
 
@@ -393,7 +399,6 @@
         all_copies(send, recv, out_send, out_recv, g).wait_send()
         all_copies(back_send, back_recv, ret_send, ret_recv, g).wait_send()
         out_copy(g).wait()
-        moved_copy(g).wait()
         return carry
 
     lax.fori_loop(0, GROUPS, finish, 0)
@@ -403,11 +408,11 @@
     hbm = pl.BlockSpec(memory_space=pltpu.HBM)
     dma = pltpu.SemaphoreType.DMA
     comps = GROUPS * NF
-    renewed, moved = pl.pallas_call(
+    return pl.pallas_call(
         step_kernel,
-        out_shape=[jax.ShapeDtypeStruct((ROWS, comps, LON), BF)] * 2,
+        out_shape=jax.ShapeDtypeStruct((ROWS, comps, LON), BF),
         in_specs=[hbm] * 6,
-        out_specs=[hbm] * 2,
+        out_specs=hbm,
         scratch_shapes=[
             pltpu.VMEM((ROWS, comps, LON), BF),
             pltpu.VMEM((ROWS, LON), F32),
@@ -423,13 +428,15 @@
             pltpu.VMEM((ROWS, comps, LON), BF),
             pltpu.VMEM((ROWS, 1, LON), F32),
             pltpu.VMEM((ROWS, 1, LON), F32),
+            pltpu.VMEM((ROWS, 1, LON), F32),
             pltpu.VMEM((ROWS, LON, LON), BF),
             pltpu.VMEM((ROWS, WINDOWS, STRIP, LON), BF),
             pltpu.VMEM((ROWS, NF, LON), BF),
             pltpu.VMEM((GROUPS, SPEC, NF, HALF), BF),
             pltpu.VMEM((GROUPS, SPEC, NF, HALF), BF),
             pltpu.VMEM((GROUPS, SPEC * NF, HALF), F32),
-            pltpu.VMEM((GROUPS * GROUPS, SPEC * NF, SPEC * NF), BF),
+            pltpu.VMEM((SPEC * NF, SPEC * NF), BF),
+            pltpu.VMEM((SPEC * NF, SPEC * NF), BF),
             pltpu.VMEM((GROUPS * 2 * SPEC, NF, HALF), BF),
             pltpu.VMEM((ND, 1, ND * NF), F32),
             pltpu.VMEM((GROUPS, SPEC, NF, HALF), BF),
@@ -445,13 +452,11 @@
             dma((5,)),
             dma((GROUPS,)),
             dma((GROUPS,)),
-            dma((GROUPS,)),
         ],
         compiler_params=pltpu.CompilerParams(
             collective_id=0, has_side_effects=True, vmem_limit_bytes=64 * 1024 * 1024
         ),
     )(action, east_current, north_current, sea_mask, pattern.T, table)
-    return jnp.where(sea_mask[:, None, :] > 0, renewed, moved)
 
 
 def solution(mesh):

time: 51.9 us -> 52.9 us (1.019)
  other arithmetic: 4.5 us -> 0 us
  Pallas kernels: 47.2 us -> 50.1 us
  local copies, waits for them, and re-layouts: 0 us -> 2.69 us
    select_n x1 -> x0, other arithmetic: 3.19 us -> none  [local(): return jnp.where(sea_mask[:, None, :] > 0, renewed, moved)]
    pallas_call x1, Pallas kernels: 47.2 us -> 50.1 us  [local(): pl.pallas_call(step_kernel, out_shape=jax.ShapeDtypeStruct((ROWS, comps,...]
    unnamed x0 -> x1, local copies, waits for them, and re-layouts: none -> 2.69 us
    gt x1 -> x0, other arithmetic: 1.3 us -> none  [local(): return jnp.where(sea_mask[:, None, :] > 0, renewed, moved)]
where the time goes in v3:
time: 52.9 us; the launch traced here: 52.8 us
  Pallas kernels  50.1 us (95%)
  local copies, waits for them, and re-layouts  2.69 us (5%)
    pallas_call x1, Pallas kernels, local(): pl.pallas_call(step_kernel, out_shape=jax.ShapeDtypeStruct((ROWS, comps,...  50.1 us
    unnamed x1, local copies, waits for them, and re-layouts  2.69 us

profile of v3, /device:TPU:8, one launch (start us, length us, event | category | flops | bytes accessed | tf_op | source)
XLA Modules:
  0.0 52.8 jit_solution(7129880261748491086)
XLA Ops:
  0.0 50.1 %shard_map.64 = bf16[16,192,256]{2,1,0:T(8,128)(2,1)} custom-call(bf16[16,192,256]{2,1,0:T(8,128)(2,1)} %action_hbm.1, f32[16,256]{1,0:T(8,128)} %east_hbm.1, f32[16,256]{1,0:T(8,128)} %north_hbm.1, s32[16,256]{1,0:T(8,128)} %mask_hbm.1, s32[24,48]{1,0:T(8,128)} %bitcast.1, bf16[48,64,64]{2,1,0:T(8,128)(2,1)} %table_hbm.1), custom_call_target="tpu_custom_call" | custom-call | tf_op jit(solution)/shard_map/pallas_call | solution.py:411
  50.1 2.7 %copy.8 = bf16[16,192,256]{2,1,0:T(8,128)(2,1)} copy(bf16[16,192,256]{2,1,0:T(8,128)(2,1)} %shard_map.64) | data formatting | bytes 3145728

commit v4 on v3

--- a/solution.py
+++ b/solution.py
@@ -359,12 +359,10 @@
 
     for q in range(SPEC):
         build_weight(0, q)
-    outgoing(0)
-    outgoing(1)
-    couple(0)
-    outgoing(2)
-    couple(1)
-    couple(2)
+    for g in range(GROUPS):
+        outgoing(g)
+    for g in range(GROUPS):
+        couple(g)
 
     def out_copy(h):
         return pltpu.make_async_copy(out.at[:, group(h)], out_hbm.at[:, group(h)], store_sem.at[h])

time: 52.9 us -> 48 us (0.907)
  Pallas kernels: 50.1 us -> 45.2 us
    pallas_call x1, Pallas kernels: 50.1 us -> 45.2 us  [local(): pl.pallas_call(step_kernel, out_shape=jax.ShapeDtypeStruct((ROWS, comps,...]
where the time goes in v4:
time: 48 us; the launch traced here: 47.9 us
  Pallas kernels  45.2 us (94%)
  local copies, waits for them, and re-layouts  2.69 us (6%)
    pallas_call x1, Pallas kernels, local(): pl.pallas_call(step_kernel, out_shape=jax.ShapeDtypeStruct((ROWS, comps,...  45.2 us
    unnamed x1, local copies, waits for them, and re-layouts  2.69 us

profile of v4, /device:TPU:8, one launch (start us, length us, event | category | flops | bytes accessed | tf_op | source)
XLA Modules:
  0.0 47.9 jit_solution(11313574800035434731)
XLA Ops:
  0.0 45.2 %shard_map.64 = bf16[16,192,256]{2,1,0:T(8,128)(2,1)} custom-call(bf16[16,192,256]{2,1,0:T(8,128)(2,1)} %action_hbm.1, f32[16,256]{1,0:T(8,128)} %east_hbm.1, f32[16,256]{1,0:T(8,128)} %north_hbm.1, s32[16,256]{1,0:T(8,128)} %mask_hbm.1, s32[24,48]{1,0:T(8,128)} %bitcast.1, bf16[48,64,64]{2,1,0:T(8,128)(2,1)} %table_hbm.1), custom_call_target="tpu_custom_call" | custom-call | tf_op jit(solution)/shard_map/pallas_call | solution.py:409
  45.2 2.7 %copy.8 = bf16[16,192,256]{2,1,0:T(8,128)(2,1)} copy(bf16[16,192,256]{2,1,0:T(8,128)(2,1)} %shard_map.64) | data formatting | bytes 3145728

commit v5 on v4

--- a/solution.py
+++ b/solution.py
@@ -34,7 +34,7 @@
 
 def step_kernel(
     action_hbm, east_hbm, north_hbm, mask_hbm, pattern_hbm, table_hbm, out_hbm,
-    action, east, north, mask, pattern, table, out, halo, current, coef_e, coef_n, moved, slot_row, window_row, mask_row, onehot, windows, ring,
+    action, east, north, mask, pattern, table, out, halo, current, coef_e, coef_n, moved, slot_row, window_row, mask_row, onehot_t, onehot, windows, ring,
     send, recv, total, weight_a, weight_b, pairs, hits, back_send, back_recv,
     halo_send, halo_recv, cur_send, cur_recv, out_send, out_recv, ret_send, ret_recv,
     load_sem, action_sem, store_sem,
@@ -147,7 +147,11 @@
     base = jnp.floor(first * (1.0 / LON))
     lane = iota((ROWS, LON), 1).astype(F32)
     window_at = base + jnp.where(lane < first - LON * base, 1.0, 0.0)
+    turned = jnp.transpose(place_at)
+    across = iota((LON, LON), 1).astype(F32)
     for row in range(ROWS):
+        column_at = jnp.broadcast_to(turned[:, row : row + 1], (LON, LON))
+        onehot_t[row] = jnp.where(column_at == across, 1.0, 0.0).astype(BF)
         slot_row[row] = place_at[row : row + 1]
         window_row[row] = window_at[row : row + 1]
         mask_row[row] = sea[row : row + 1]
@@ -283,22 +287,26 @@
             device_id={"spec": lax.rem(me + 1, SPEC)}, device_id_type=MESH,
         )
 
-    def outgoing(g):
+    def squeeze(g, row):
+        lines = moved[row, g * NF : (g + 1) * NF, :]
+        ring[row] = dot(lines, onehot_t[row]).astype(BF)
+
+    def advance(g):
         to_up, to_down = halo_copies(g)
         action_copy(g).wait()
         to_up.wait()
         to_down.wait()
-        comps = group(g)
 
         def strip(s, inner):
+            if g > 0:
+                for k in range(ROWS * STRIP // NF):
+                    squeeze(g - 1, s * (ROWS * STRIP // NF) + k)
             propagate(pl.multiple_of(g * NF + s * STRIP, STRIP))
             return inner
 
         lax.fori_loop(0, NF // STRIP, strip, 0)
 
-        for row in range(ROWS):
-            ring[row] = dot(moved[row, comps, :], onehot[row], 1, 1).astype(BF)
-
+    def outgoing(g):
         def gather(w, inner):
             for s in range(NF // STRIP):
                 rows = slice(s * STRIP, (s + 1) * STRIP)
@@ -360,7 +368,12 @@
     for q in range(SPEC):
         build_weight(0, q)
     for g in range(GROUPS):
-        outgoing(g)
+        advance(g)
+        if g > 0:
+            outgoing(g - 1)
+    for row in range(ROWS):
+        squeeze(GROUPS - 1, row)
+    outgoing(GROUPS - 1)
     for g in range(GROUPS):
         couple(g)
 
@@ -428,6 +441,7 @@
             pltpu.VMEM((ROWS, 1, LON), F32),
             pltpu.VMEM((ROWS, 1, LON), F32),
             pltpu.VMEM((ROWS, LON, LON), BF),
+            pltpu.VMEM((ROWS, LON, LON), BF),
             pltpu.VMEM((ROWS, WINDOWS, STRIP, LON), BF),
             pltpu.VMEM((ROWS, NF, LON), BF),
             pltpu.VMEM((GROUPS, SPEC, NF, HALF), BF),

time: 48 us -> 48.1 us (level)
  no operation moved by 1% of the time
where the time goes in v5:
time: 48.1 us; the launch traced here: 48 us
  Pallas kernels  45.3 us (94%)
  local copies, waits for them, and re-layouts  2.69 us (6%)
    pallas_call x1, Pallas kernels, local(): pl.pallas_call(step_kernel, out_shape=jax.ShapeDtypeStruct((ROWS, comps,...  45.3 us
    unnamed x1, local copies, waits for them, and re-layouts  2.69 us

profile of v5, /device:TPU:8, one launch (start us, length us, event | category | flops | bytes accessed | tf_op | source)
XLA Modules:
  0.0 48.0 jit_solution(16714350759539810676)
XLA Ops:
  0.0 45.3 %shard_map.64 = bf16[16,192,256]{2,1,0:T(8,128)(2,1)} custom-call(bf16[16,192,256]{2,1,0:T(8,128)(2,1)} %action_hbm.1, f32[16,256]{1,0:T(8,128)} %east_hbm.1, f32[16,256]{1,0:T(8,128)} %north_hbm.1, s32[16,256]{1,0:T(8,128)} %mask_hbm.1, s32[24,48]{1,0:T(8,128)} %bitcast.1, bf16[48,64,64]{2,1,0:T(8,128)(2,1)} %table_hbm.1), custom_call_target="tpu_custom_call" | custom-call | tf_op jit(solution)/shard_map/pallas_call | solution.py:422
  45.3 2.7 %copy.8 = bf16[16,192,256]{2,1,0:T(8,128)(2,1)} copy(bf16[16,192,256]{2,1,0:T(8,128)(2,1)} %shard_map.64) | data formatting | bytes 3145728
